TPU v7x, 32 devices: a whole 2x2x4 slice. The times are simulated.
32 devices in a mesh: dp: 8 (over z, y), head: 4 (over x, core).
Axes of the slice: x: 2, y: 2, z: 4, core: 2. Of those that a mesh axis runs over, the one named last changes fastest.
Arguments:
- inputs: bfloat16 [8192, 2048], P('dp', 'head'), may hold values from -6 to 6
- cotangent: bfloat16 [8192, 2048], P('dp', 'head'), may hold values from -6 to 6
- token_valid: int32 [8192], P('dp'), may hold values from 0 to 1, as said below
- block_opens: int32 [32], P('dp'), may hold values from 0 to 1, as said below
- block_widths: int32 [32], P('dp'), may hold values from 16 to 64, as said below
- weight_inner: float32 [2048, 2, 4096], P('dp', None, 'head'), may hold values from -0.125 to 0.125
- weight_step: float32 [2048, 64], P('dp', 'head'), may hold values from -0.125 to 0.125
- weight_output: float32 [4096, 2048], P('head', 'dp'), may hold values from -0.09375 to 0.09375
- weight_state: float32 [2048, 256], P(('dp', 'head')), may hold values from -0.125 to 0.125
- norm_gain: float32 [2048], P(('dp', 'head')), may hold values from 0.5 to 1.5
- channel_table: float32 [6, 4096], P(None, 'head'), may hold values from -1.5 to 1.5, as said below
- head_table: float32 [3, 64], P(None, 'head'), may hold values from -9 to 1.5
- state_filter: float32 [256, 5], P(('dp', 'head')), may hold values from -2.5 to 2.5
- momentum_inner: float32 [2048, 2, 4096], P('dp', None, 'head'), may hold values from -112 to 112
- momentum_step: float32 [2048, 64], P('dp', 'head'), may hold values from -160 to 160
- momentum_output: float32 [4096, 2048], P('head', 'dp'), may hold values from -256 to 256
- momentum_state: float32 [2048, 256], P(('dp', 'head')), may hold values from -56 to 56
- momentum_gain: float32 [2048], P(('dp', 'head')), may hold values from -512 to 512
- momentum_channel: float32 [6, 4096], P(None, 'head'), may hold values from -256 to 256
- momentum_head: float32 [3, 64], P(None, 'head'), may hold values from -1024 to 1024
- momentum_filter: float32 [256, 5], P(('dp', 'head')), may hold values from -256 to 256
- average_inner: float32 [2048, 2, 4096], P('dp', None, 'head'), may hold values from -0.125 to 0.125
- average_step: float32 [2048, 64], P('dp', 'head'), may hold values from -0.125 to 0.125
- average_output: float32 [4096, 2048], P('head', 'dp'), may hold values from -0.09375 to 0.09375
- average_state: float32 [2048, 256], P(('dp', 'head')), may hold values from -0.125 to 0.125
- average_gain: float32 [2048], P(('dp', 'head')), may hold values from 0.5 to 1.5
- average_channel: float32 [6, 4096], P(None, 'head'), may hold values from -3 to 3
- average_head: float32 [3, 64], P(None, 'head'), may hold values from -6 to 6
- average_filter: float32 [256, 5], P(('dp', 'head')), may hold values from -3 to 3
Outputs:
- layer_output: bfloat16 [8192, 2048], P('dp', 'head')
- grad_input: float32 [8192, 2048], P('dp', 'head')
- updated_inner: float32 [2048, 2, 4096], P('dp', None, 'head')
- carried_inner: float32 [2048, 2, 4096], P('dp', None, 'head')
- smoothed_inner: float32 [2048, 2, 4096], P('dp', None, 'head')
- updated_step: float32 [2048, 64], P('dp', 'head')
- carried_step: float32 [2048, 64], P('dp', 'head')
- smoothed_step: float32 [2048, 64], P('dp', 'head')
- updated_output: float32 [4096, 2048], P('head', 'dp')
- carried_output: float32 [4096, 2048], P('head', 'dp')
- smoothed_output: float32 [4096, 2048], P('head', 'dp')
- updated_state: float32 [2048, 256], P(('dp', 'head'))
- carried_state: float32 [2048, 256], P(('dp', 'head'))
- smoothed_state: float32 [2048, 256], P(('dp', 'head'))
- updated_gain: float32 [2048], P(('dp', 'head'))
- carried_gain: float32 [2048], P(('dp', 'head'))
- smoothed_gain: float32 [2048], P(('dp', 'head'))
- updated_channel: float32 [6, 4096], P(None, 'head')
- carried_channel: float32 [6, 4096], P(None, 'head')
- smoothed_channel: float32 [6, 4096], P(None, 'head')
- updated_head: float32 [3, 64], P(None, 'head')
- carried_head: float32 [3, 64], P(None, 'head')
- smoothed_head: float32 [3, 64], P(None, 'head')
- updated_filter: float32 [256, 5], P(('dp', 'head'))
- carried_filter: float32 [256, 5], P(('dp', 'head'))
- smoothed_filter: float32 [256, 5], P(('dp', 'head'))
Inputs may be any that keep to these rules, and one draw needn't show every extreme that they name: `block_opens`: the first block of each index of dp's 1024 tokens begins a sequence; some index of dp holds one sequence of all its 1024 tokens. `block_widths`: the same for all blocks of a sequence, a multiple of 16. `token_valid`: 1 on a prefix of each sequence that covers all its blocks but the last, and 128 or more tokens of the last; 0 on the rest of that block. `channel_table`: rows 0 to 3 taps, row 4 biases, row 5 gains.
All inputs are finite; a program needn't handle non-finite values.
Results may differ from a plain program's by a relative error of at most 0.0095.
The roundings to bfloat16 on the way count: a program that leaves them out, or rounds other values in their place, can miss the bound.
Values may be sent and summed in bfloat16 or wider, within the bound.
No kernel may reach another device: no remote copies, remote signals or barrier semaphores. Data moves between devices by JAX's collectives and lax.ppermute only.
A program may use at most 192 MiB of HBM per device.

v0:
```python
import math
import jax
import jax.numpy as jnp
from jax import lax
from jax.sharding import PartitionSpec as P

D = 2048
H = 64
P_SIZE = 64
NS = 128
KC = 4
BLK = 256
EPS = 1e-05
MOMENTUM = 0.9
DECAY = 0.0001
AVERAGE = 0.75
RATE_MATRIX = 0.02
RATE_VECTOR = 0.1
HIGHEST = lax.Precision.HIGHEST


def rounded(value):
    return lax.optimization_barrier(value.astype(jnp.bfloat16)).astype(jnp.float32)


def convolve(inner_x, state_bc, taps_x, taps_bc, openings):
    joined = jnp.concatenate([inner_x, state_bc], axis=1)
    filters = jnp.concatenate([taps_x, taps_bc], axis=1)
    within = jnp.arange(joined.shape[0]) % BLK
    conv_total = filters[KC][None, :] + filters[KC - 1][None, :] * joined
    for offset in range(1, KC):
        shifted = jnp.concatenate(
            [jnp.zeros((offset, joined.shape[1]), jnp.float32), joined[:-offset]], axis=0
        )
        allowed = 1.0 - openings * (within < offset).astype(jnp.float32)
        conv_total = conv_total + filters[KC - 1 - offset][None, :] * shifted * allowed[:, None]
    active = jax.nn.silu(conv_total)
    split_at = inner_x.shape[1]
    return (active[:, :split_at], active[:, split_at:])


def state_mixer(signal_x, signal_bc, step_raw, gate_values, table, head_used, block_open):
    token_count, channels = signal_x.shape
    heads_here = table.shape[1]
    blocks_here = token_count // BLK
    step_rates = jax.nn.softplus(step_raw + table[0][None, :])
    log_rates = step_rates * (-jnp.exp(table[1]))[None, :]
    cumulated = jnp.cumsum(log_rates.reshape(blocks_here, BLK, heads_here), axis=1)
    rates_block = step_rates.reshape(blocks_here, BLK, heads_here)
    values = signal_x.reshape(blocks_here, BLK, heads_here, P_SIZE)
    inputs_map = signal_bc[:, :NS].reshape(blocks_here, BLK, NS)
    outputs_map = signal_bc[:, NS:].reshape(blocks_here, BLK, NS)
    lower_mask = (jnp.arange(BLK)[:, None] >= jnp.arange(BLK)[None, :])[None, :, :, None]
    spread = cumulated[:, :, None, :] - cumulated[:, None, :, :]
    decays = jnp.where(lower_mask, jnp.exp(jnp.where(lower_mask, spread, 0.0)), 0.0)
    intersection = jnp.einsum("nts,nus->ntu", outputs_map, inputs_map, precision=HIGHEST)
    mixing = intersection[..., None] * decays * rates_block[:, None, :, :]
    inner_part = jnp.einsum("ntuh,nuhp->nthp", mixing, values, precision=HIGHEST)
    ending = jnp.exp(cumulated[:, -1:, :] - cumulated) * rates_block
    pieces = jnp.einsum("nuh,nuhp,nus->nhps", ending, values, inputs_map, precision=HIGHEST)
    totals = jnp.exp(cumulated[:, -1, :])

    def carry_state(state_now, entries):
        piece_state, total_decay, opening = entries
        entering = state_now * (1.0 - opening)
        return (total_decay[:, None, None] * entering + piece_state, entering)

    initial = jnp.zeros((heads_here, P_SIZE, NS), jnp.float32)
    finals, entered = lax.scan(carry_state, initial, (pieces, totals, block_open))
    outer_part = jnp.exp(cumulated)[..., None] * jnp.einsum(
        "nhps,nts->nthp", entered, outputs_map, precision=HIGHEST
    )
    mixed = (inner_part + outer_part + table[2][None, None, :, None] * values) * head_used.reshape(
        blocks_here, BLK, heads_here
    )[..., None]
    gated = mixed.reshape(token_count, channels) * jax.nn.silu(gate_values)
    return (gated, jnp.sum(gated * gated, axis=1))


def gated_norm(gated, total_sq, gate_gain, norm_counts):
    norm_scale = lax.rsqrt(total_sq / norm_counts + EPS)
    return gated * norm_scale[:, None] * gate_gain[None, :]


def advance(weight, gradient, moment, average, rate):
    adjusted = gradient + DECAY * weight
    moment_next = MOMENTUM * moment + adjusted
    weight_next = weight - rate * (adjusted + MOMENTUM * moment_next)
    average_next = AVERAGE * average + (1.0 - AVERAGE) * weight_next
    return (weight_next, moment_next, average_next)


def body(
    inputs,
    cotangent,
    token_valid,
    block_opens,
    block_widths,
    weight_inner,
    weight_step,
    weight_output,
    weight_state,
    norm_gain,
    channel_table,
    head_table,
    state_filter,
    momentum_inner,
    momentum_step,
    momentum_output,
    momentum_state,
    momentum_gain,
    momentum_channel,
    momentum_head,
    momentum_filter,
    average_inner,
    average_step,
    average_output,
    average_state,
    average_gain,
    average_channel,
    average_head,
    average_filter,
):
    inner_full, step_full, output_full = (
        lax.all_gather(weight_inner.astype(jnp.bfloat16), "dp", axis=0, tiled=True),
        lax.all_gather(weight_step.astype(jnp.bfloat16), "dp", axis=0, tiled=True),
        lax.all_gather(weight_output.astype(jnp.bfloat16), "dp", axis=1, tiled=True),
    )
    state_full, gain_full, filter_full = (
        lax.all_gather(weight_state.astype(jnp.bfloat16), ("dp", "head"), axis=0, tiled=True),
        lax.all_gather(norm_gain.astype(jnp.bfloat16), ("dp", "head"), axis=0, tiled=True),
        lax.all_gather(state_filter.astype(jnp.bfloat16), ("dp", "head"), axis=0, tiled=True),
    )
    channel_used = rounded(channel_table)
    head_values = rounded(head_table)
    gathered = lax.all_gather(inputs, "head", axis=1, tiled=True)
    tokens_full = gathered.astype(jnp.float32)
    inverse = lax.rsqrt(jnp.mean(tokens_full * tokens_full, axis=1) + EPS)
    gain_float = gain_full.astype(jnp.float32)
    normed = (tokens_full * inverse[:, None] * gain_float[None, :]).astype(jnp.bfloat16)
    inner_pair = jnp.einsum("td,dkc->tkc", normed, inner_full, preferred_element_type=jnp.float32)
    gate_values = inner_pair[:, 0]
    inner_x = inner_pair[:, 1]
    state_bc = jnp.dot(normed, state_full, preferred_element_type=jnp.float32)
    step_raw = jnp.dot(normed, step_full, preferred_element_type=jnp.float32)
    block_open = block_opens.astype(jnp.float32)
    openings = jnp.repeat(block_open, BLK)
    widths = jnp.repeat(block_widths, BLK)
    heads_local = step_full.shape[1]
    head_used = (jnp.arange(heads_local)[None, :] * H < widths[:, None] * heads_local).astype(
        jnp.float32
    )
    norm_counts = widths.astype(jnp.float32) * P_SIZE
    valid_rows = token_valid.astype(jnp.float32)
    taps_x = channel_used[: KC + 1]
    gate_gain = channel_used[KC + 1]
    taps_bc = filter_full.astype(jnp.float32).T

    def conv_part(inner_value, state_value, taps_first, taps_second):
        return convolve(inner_value, state_value, taps_first, taps_second, openings)

    (conv_x, conv_bc), conv_back = jax.vjp(conv_part, inner_x, state_bc, taps_x, taps_bc)
    signal_x = rounded(conv_x)
    signal_bc = rounded(conv_bc)

    def mix_part(signal_first, signal_second, raw_steps, gate_part, table):
        return state_mixer(
            signal_first, signal_second, raw_steps, gate_part, table, head_used, block_open
        )

    (gated, local_sq), mix_back = jax.vjp(
        mix_part, signal_x, signal_bc, step_raw, gate_values, head_values
    )
    total_sq = lax.psum(local_sq, "head")

    def norm_part(gated_value, sum_value, gain_value):
        return gated_norm(gated_value, sum_value, gain_value, norm_counts)

    normalized, norm_back_fn = jax.vjp(norm_part, gated, total_sq, gate_gain)
    projected = normalized.astype(jnp.bfloat16)
    partial_out = jnp.dot(projected, output_full, preferred_element_type=jnp.float32)
    branch = lax.psum_scatter(
        partial_out.astype(jnp.bfloat16), "head", scatter_dimension=1, tiled=True
    ).astype(jnp.float32)
    own_inputs = inputs.astype(jnp.float32)
    layer_output = (own_inputs + valid_rows[:, None] * branch).astype(jnp.bfloat16)
    masked = cotangent * token_valid.astype(jnp.bfloat16)[:, None]
    shard_piece = lax.all_gather(masked, "head", axis=1, tiled=True)
    grad_normal = jnp.einsum(
        "tw,cw->tc", shard_piece, output_full, preferred_element_type=jnp.float32
    )
    block_grad = jnp.einsum("tc,tw->cw", projected, shard_piece, preferred_element_type=jnp.float32)
    grad_gated, grad_sq_part, grad_gate_gain = norm_back_fn(grad_normal)
    grad_sq = lax.psum(grad_sq_part, "head")
    grad_sx, grad_sbc, grad_raw, grad_gate, grad_head = mix_back((grad_gated, grad_sq))
    grad_inner_x, grad_state_bc, grad_taps_x, grad_taps_bc = conv_back((grad_sx, grad_sbc))
    pair_low = jnp.stack([grad_gate, grad_inner_x], axis=1).astype(jnp.bfloat16)
    state_low = grad_state_bc.astype(jnp.bfloat16)
    step_low = grad_raw.astype(jnp.bfloat16)
    grad_inner = jnp.einsum("td,tkc->dkc", normed, pair_low, preferred_element_type=jnp.float32)
    grad_state = jnp.einsum("td,ts->ds", normed, state_low, preferred_element_type=jnp.float32)
    grad_step = jnp.einsum("td,th->dh", normed, step_low, preferred_element_type=jnp.float32)
    grad_normed = jnp.einsum(
        "tkc,dkc->td", pair_low, inner_full, preferred_element_type=jnp.float32
    )
    grad_normed = grad_normed + jnp.einsum(
        "ts,ds->td", state_low, state_full, preferred_element_type=jnp.float32
    )
    grad_normed = grad_normed + jnp.einsum(
        "th,dh->td", step_low, step_full, preferred_element_type=jnp.float32
    )
    own_grad = lax.psum_scatter(
        grad_normed.astype(jnp.bfloat16), "head", scatter_dimension=1, tiled=True
    ).astype(jnp.float32)
    own_width = inputs.shape[1]
    start_column = lax.axis_index("head") * own_width
    own_gain = lax.dynamic_slice_in_dim(gain_float, start_column, own_width)
    scaled = own_grad * own_gain[None, :]
    row_part = jnp.sum(scaled * own_inputs, axis=1)
    grad_gain_own = jnp.sum(own_grad * own_inputs * inverse[:, None], axis=0)
    row_total = lax.psum(row_part, "head")
    inverse_cube = inverse * inverse * inverse
    grad_input = (
        cotangent.astype(jnp.float32)
        + inverse[:, None] * scaled
        - own_inputs * (inverse_cube * row_total / D)[:, None]
    )
    grad_gain_full = lax.dynamic_update_slice_in_dim(
        jnp.zeros((D,), jnp.float32), grad_gain_own, start_column, 0
    )
    grad_channel = jnp.concatenate([grad_taps_x, grad_gate_gain[None, :]], axis=0)
    grad_filter = grad_taps_bc.T
    inner_reduced, step_reduced, output_reduced = (
        lax.psum_scatter(grad_inner, "dp", scatter_dimension=0, tiled=True),
        lax.psum_scatter(grad_step, "dp", scatter_dimension=0, tiled=True),
        lax.psum_scatter(block_grad, "dp", scatter_dimension=1, tiled=True),
    )
    state_reduced, gain_reduced, filter_reduced = (
        lax.psum_scatter(grad_state, ("dp", "head"), scatter_dimension=0, tiled=True),
        lax.psum_scatter(grad_gain_full, ("dp", "head"), scatter_dimension=0, tiled=True),
        lax.psum_scatter(grad_filter, ("dp", "head"), scatter_dimension=0, tiled=True),
    )
    channel_reduced, head_reduced = lax.psum((grad_channel, grad_head), "dp")
    total_tokens = inputs.shape[0] * lax.axis_size("dp")
    matrix_rate = RATE_MATRIX / math.sqrt(total_tokens)
    vector_rate = RATE_VECTOR / math.sqrt(total_tokens)
    new_inner = advance(weight_inner, inner_reduced, momentum_inner, average_inner, matrix_rate)
    new_step = advance(weight_step, step_reduced, momentum_step, average_step, matrix_rate)
    new_output = advance(
        weight_output, output_reduced, momentum_output, average_output, matrix_rate
    )
    new_state = advance(weight_state, state_reduced, momentum_state, average_state, matrix_rate)
    new_gain = advance(norm_gain, gain_reduced, momentum_gain, average_gain, vector_rate)
    new_channel = advance(
        channel_table, channel_reduced, momentum_channel, average_channel, vector_rate
    )
    new_head = advance(head_table, head_reduced, momentum_head, average_head, vector_rate)
    new_filter = advance(state_filter, filter_reduced, momentum_filter, average_filter, vector_rate)
    return (
        layer_output,
        grad_input,
        new_inner[0],
        new_inner[1],
        new_inner[2],
        new_step[0],
        new_step[1],
        new_step[2],
        new_output[0],
        new_output[1],
        new_output[2],
        new_state[0],
        new_state[1],
        new_state[2],
        new_gain[0],
        new_gain[1],
        new_gain[2],
        new_channel[0],
        new_channel[1],
        new_channel[2],
        new_head[0],
        new_head[1],
        new_head[2],
        new_filter[0],
        new_filter[1],
        new_filter[2],
    )


def solution(mesh):
    in_specs = (
        P("dp", "head"),
        P("dp", "head"),
        P("dp"),
        P("dp"),
        P("dp"),
        P("dp", None, "head"),
        P("dp", "head"),
        P("head", "dp"),
        P(("dp", "head"), None),
        P(("dp", "head")),
        P(None, "head"),
        P(None, "head"),
        P(("dp", "head"), None),
        P("dp", None, "head"),
        P("dp", "head"),
        P("head", "dp"),
        P(("dp", "head"), None),
        P(("dp", "head")),
        P(None, "head"),
        P(None, "head"),
        P(("dp", "head"), None),
        P("dp", None, "head"),
        P("dp", "head"),
        P("head", "dp"),
        P(("dp", "head"), None),
        P(("dp", "head")),
        P(None, "head"),
        P(None, "head"),
        P(("dp", "head"), None),
    )
    out_specs = (
        P("dp", "head"),
        P("dp", "head"),
        P("dp", None, "head"),
        P("dp", None, "head"),
        P("dp", None, "head"),
        P("dp", "head"),
        P("dp", "head"),
        P("dp", "head"),
        P("head", "dp"),
        P("head", "dp"),
        P("head", "dp"),
        P(("dp", "head"), None),
        P(("dp", "head"), None),
        P(("dp", "head"), None),
        P(("dp", "head")),
        P(("dp", "head")),
        P(("dp", "head")),
        P(None, "head"),
        P(None, "head"),
        P(None, "head"),
        P(None, "head"),
        P(None, "head"),
        P(None, "head"),
        P(("dp", "head"), None),
        P(("dp", "head"), None),
        P(("dp", "head"), None),
    )
    return jax.shard_map(body, mesh=mesh, in_specs=in_specs, out_specs=out_specs, check_vma=False)
```

profile of v0, /device:TPU:0, one launch (start us, length us, event | category | flops | bytes accessed | tf_op | source)
XLA Modules:
  0.0 1316.8 jit_solution(10096558258720219206)
XLA Ops:
  16.7 42.3 %all-reduce.20 = bf16[2048]{0:T(1024)(128)(2,1)S(1)} all-reduce(bf16[2048]{0:T(1024)(128)(2,1)S(1)} %dynamic-update-slice), channel_id=1, replica_groups=mesh['dp'=8,'head'=4] {'dp','head'}, use_global_device_ids=true, to_apply=%add.20 | all-reduce | flops 2048 | bytes 8192
  59.1 40.5 %all_gather.24 = bf16[256,5]{1,0:T(8,128)(2,1)S(1)} all-gather(bf16[8,5]{1,0:T(8,128)(2,1)S(1)} %convert_element_type.103), channel_id=1, replica_groups=mesh['dp'=8,'head'=4] {'dp','head'}, dimensions={0}, use_global_device_ids=true | all-gather | bytes 2640 | tf_op jit(solution)/shard_map/all_gather | solution.py:132
  104.6 7.7 reshape.331
  112.9 30.9 %all_gather.29 = bf16[2048,16]{0,1:T(8,128)(2,1)S(1)} all-gather(bf16[256,16]{0,1:T(8,128)(2,1)S(1)} %convert_element_type.111), channel_id=1, replica_groups=mesh['dp'=8,'head'=4] {'dp'}, dimensions={0}, use_global_device_ids=true | all-gather | bytes 73728 | tf_op jit(solution)/shard_map/all_gather | solution.py:126
  162.0 70.0 %all-gather.8.cloned.1.call-done = bf16[2048,2,1024]{2,0,1:T(8,128)(2,1)} async-done(((bf16[256,2,1024]{2,0,1:T(8,128)(2,1)}), bf16[2048,2,1024]{2,0,1:T(8,128)(2,1)}) %all-gather.8.cloned.1.call-update) | async-done | bytes 8388624 | tf_op jit(solution)/shard_map/all_gather | solution.py:125
  231.9 12.5 fusion.50
  256.1 8.3 multiply_convert_fusion
  280.1 7.7 copy.278
  287.9 7.7 copy.273
  307.2 23.2 %while.36 = (s32[]{:T(128)}, f32[16,64,128]{2,1,0:T(8,128)S(1)}, f32[4,16,64,128]{3,2,1,0:T(8,128)S(1)}, f32[4]{0:T(128)}, f32[4,16,1,1]{1,3,2,0:T(1,128)}, /*in...) while((s32[]{:T(128)}, f32[16,64,128]{2,1,0:T(8,128)S(1)}, ...), condition=%wide.region_4.5_spmd.clone, body=%wide.region_3.4_spmd.clone.sunk | while | flops 786436 | bytes 2622828 | solution.py:69
  333.4 18.0 %multiply_reduce_fusion.10 = (f32[4,256]{1,0:T(4,128)S(1)}, f32[4,256,16,64]{1,3,2,0:T(8,128)}) fusion(f32[4,256,16,64]{1,3,2,0:T(8,128)S(1)} %copy-done.25, f32[4,256,16]{1,2,0:T(8,128)S(1)} %compare_convert_fusion, f32[4,256,16,64]{1,3,2,0:T(8,128)} %copy.273, f32[16]{0:T(128)S(1)} %copy-done.99, f32[4,256,16,64]{1,3,2,0:T(8,128)S(1)} %fusion.139, ...), kind=kOutput, calls=%fused_computation.102 | convolution fusion | flops 3254778880 | bytes 20254784 | tf_op jit(solution)/shard_map/jvp(ntuh,nuhp->nthp)/dot_general | solution.py:58
  351.4 8.2 copy.333
  359.6 7.6 reshape.334
  373.9 14.9 %multiply_reduce_fusion.7 = (f32[1024]{0:T(1024)}, f32[1024]{0:T(1024)S(1)}, f32[1024,1024]{1,0:T(8,128)}, f32[1024,1024]{1,0:T(8,128)}) fusion(f32[1024]{0:T(1024)S(1)} %fusion.121, f32[1024]{0:T(1024)S(1)} %bitcast.298, f32[1024,1024]{1,0:T(8,128)} %reshape.334, f32[1024,2,1024]{2,0,1:T(8,128)} %copy-done.11, ...), kind=kOutput, calls=%fused_computation.98 | convolution fusion | flops 4306499584 | bytes 25182208 | tf_op jit(solution)/shard_map/tw,cw->tc/dot_general | solution.py:189
  394.8 12.6 multiply_reduce_fusion.6
  414.6 7.7 copy.281
  429.7 16.3 %while.37 = (s32[]{:T(128)}, f32[16,64,128]{2,1,0:T(8,128)S(1)}, f32[4,16,64,128]{3,2,1,0:T(8,128)}, f32[4,16]{1,0:T(4,128)S(1)}, f32[4,16,64,128]{3,2,1,0:T(8,1...) while((s32[]{:T(128)}, f32[16,64,128]{2,1,0:T(8,128)S(1)}, ...), condition=%wide.region_13.14_spmd.clone, body=%wide.region_11.13_spmd.clone.sunk | while | flops 917492 | bytes 3146284 | solution.py:69
  457.3 22.5 %fusion.14 = (f32[4,256,16]{1,2,0:T(8,128)}, f32[4,256,16]{1,2,0:T(8,128)}, f32[4,256,16]{1,2,0:T(8,128)}, f32[4,256,256]{2,1,0:T(8,128)}) fusion(f32[4,256,16]{1,2,0:T(8,128)S(1)} %bitcast.307, f32[4,256,16]{1,2,0:T(8,128)S(1)} %copy-done.44, f32[4,256,256]{2,1,0:T(8,128)S(1)} %copy-done.37, pred[256,256]{1,0:T(8,128)(4,1)S(1)} %copy-done.68, ...), kind=kOutput, calls=%fused_computation.33 | convolution fusion | flops 3284877312 | bytes 8847360 | tf_op jit(solution)/shard_map/transpose(jvp(ntuh,nuhp->nthp))/dot_general | solution.py:58
  487.3 17.0 %bitcast_add_fusion.3 = f32[4,256,16,64]{1,3,2,0:T(8,128)} fusion(f32[4,256,16,64]{1,3,2,0:T(8,128)S(1)} %fusion.140, f32[4,256,16,64]{1,3,2,0:T(8,128)S(1)} %copy-done.1, f32[4,256,16]{1,2,0:T(8,128)S(1)} %bitcast.308, f32[4,256,16]{1,2,0:T(8,128)S(1)} %copy-done.44, f32[4,256,256]{2,1,0:T(8,128)S(1)} %copy-done.37, pred[256,256]{1,0:T(8,128)(4,1)S(1)} %copy-done.68, ...), kind=kOutput, calls=%fused_computation.79 | convolution fusion | flops 3248488448 | bytes 13959232 | tf_op jit(solution)/shard_map/transpose(jvp(ntuh,nuhp->nthp))/dot_general | solution.py:58
  509.5 8.1 copy.328
  555.2 9.9 reduce-window.16
  569.2 9.8 multiply_reduce_fusion.1
  588.1 11.5 fusion.66
  603.1 10.1 convolution_convert_fusion
  613.2 11.5 fusion.128
  624.8 15.4 %fusion.48 = f32[2048,2,1024]{2,0,1:T(8,128)} fusion(bf16[1024,2048]{1,0:T(8,128)(2,1)} %copy-done.5, bf16[1024,1,1024]{2,0,1:T(8,128)(2,1)} %copy-done.33, bf16[1024,1,1024]{2,0,1:T(8,128)(2,1)S(1)} %copy-done.32), kind=kOutput, calls=%fused_computation.92 | convolution fusion | flops 8598323200 | bytes 25165824 | tf_op jit(solution)/shard_map/td,tkc->dkc/dot_general | solution.py:200
  642.2 35.1 %all-reduce.24 = (f32[6,1024]{1,0:T(8,128)S(1)}, f32[3,16]{1,0:T(4,128)S(1)}) all-reduce(f32[6,1024]{1,0:T(8,128)S(1)} %pad_maximum_fusion.4, f32[3,16]{1,0:T(4,128)S(1)} %pad_add_fusion.2), channel_id=1, replica_groups=mesh['dp'=8,'head'=4] {'dp'}, use_global_device_ids=true, to_apply=%region_36.37 | all-reduce | flops 6192 | bytes 49536 | tf_op jit(solution)/shard_map/psum | solution.py:243
  679.9 87.0 %reduce-scatter.18.cloned.1.call-done = f32[64,256]{1,0:T(8,128)} async-done(((f32[2048,256]{1,0:T(8,128)}), f32[64,256]{1,0:T(8,128)}) %reduce-scatter.18.cloned.1.call-update) | async-done | bytes 65552 | tf_op jit(solution)/shard_map/reduce_scatter | solution.py:239
  768.4 41.6 %reduce-scatter.10.cloned.1.call-done = bf16[1024,512]{1,0:T(8,128)(2,1)} async-done(((bf16[1024,2048]{1,0:T(8,128)(2,1)}), bf16[1024,512]{1,0:T(8,128)(2,1)}) %reduce-scatter.10.cloned.1.call-update) | async-done | bytes 1048592 | tf_op jit(solution)/shard_map/reduce_scatter | solution.py:212
  812.5 39.7 %all-reduce.23 = (f32[2048]{0:T(1024)S(1)}, f32[256,5]{0,1:T(8,128)S(1)}) all-reduce(f32[2048]{0:T(1024)S(1)} %dynamic_update_slice.34, f32[256,5]{0,1:T(8,128)S(1)} %add_bitcast_fusion.4), channel_id=8, replica_groups=mesh['dp'=8,'head'=4] {'dp','head'}, use_global_device_ids=true, to_apply=%region_29.30.clone | all-reduce | flops 3328 | bytes 26624
  865.1 146.0 %reduce-scatter.16.cloned.1.call-done = f32[1024,256]{1,0:T(8,128)} async-done(((f32[1024,2048]{1,0:T(8,128)}), f32[1024,256]{1,0:T(8,128)}) %reduce-scatter.16.cloned.1.call-update) | async-done | bytes 1048592 | tf_op jit(solution)/shard_map/reduce_scatter | solution.py:236
  1015.0 280.9 %reduce-scatter.12.cloned.1.call-done = f32[256,2,1024]{2,0,1:T(8,128)} async-done(((f32[2048,2,1024]{2,0,1:T(8,128)}), f32[256,2,1024]{2,0,1:T(8,128)}) %reduce-scatter.12.cloned.1.call-update) | async-done | bytes 2097168 | tf_op jit(solution)/shard_map/reduce_scatter | solution.py:234
  (440 shorter events, 258.2 us)
Async XLA Ops:
  7.2 136.8 %all-gather.6.cloned.1.call-start = ((), (), s32[]{:S(2)}) async-start(), calls=%async_computation.6 | async-start | bytes 5242880 | tf_op jit(solution)/shard_map/all_gather | solution.py:136
  8.0 149.3 %all-gather.10.cloned.1.call-start = ((), (), s32[]{:S(2)}) async-start(), calls=%async_computation.8 | async-start | bytes 1081344 | tf_op jit(solution)/shard_map/all_gather | solution.py:130
  9.6 49.5 %copy-start.86 = (f32[8,5]{1,0:T(8,128)S(1)}, f32[8,5]{1,0:T(8,128)}, u32[]{:S(2)}) copy-start(f32[8,5]{1,0:T(8,128)} %param.45) | copy-start | bytes 484
  9.6 222.4 %all-gather.8.cloned.1.call-start = ((), (), s32[]{:S(2)}) async-start(), calls=%async_computation.7 | async-start | bytes 9437184 | tf_op jit(solution)/shard_map/all_gather | solution.py:125
  12.8 361.1 %all-gather.14.cloned.1.call-start = ((), (), s32[]{:S(2)}) async-start(), calls=%async_computation.11 | async-start | bytes 5242880 | tf_op jit(solution)/shard_map/all_gather | solution.py:188
  14.6 359.2 %all-gather.12.cloned.1.call-start = ((), (), s32[]{:S(2)}) async-start(), calls=%async_computation.9 | async-start | bytes 4718592 | tf_op jit(solution)/shard_map/all_gather | solution.py:127
  15.6 663.0 %reduce-scatter.14.cloned.1.call-start = ((), (), s32[]{:S(2)}) async-start(), calls=%async_computation.14 | async-start | bytes 147456 | tf_op jit(solution)/shard_map/reduce_scatter | solution.py:235
  59.1 194.3 %copy-start.72 = (f32[1024]{0:T(1024)}, f32[1024]{0:T(1024)S(1)}, u32[]{:S(2)}) copy-start(f32[1024]{0:T(1024)S(1)} %get-tuple-element.532) | copy-start | bytes 12292
  59.1 194.3 %copy-start.74 = (f32[1024]{0:T(1024)}, f32[1024]{0:T(1024)S(1)}, u32[]{:S(2)}) copy-start(f32[1024]{0:T(1024)S(1)} %get-tuple-element.534) | copy-start | bytes 12292
  143.9 109.5 %copy-start.51 = (f32[1280]{0:T(1024)}, f32[1280]{0:T(1024)S(1)}, u32[]{:S(2)}) copy-start(f32[1280]{0:T(1024)S(1)} %get-tuple-element.434) | copy-start | bytes 15364
  143.9 109.5 %copy-start.53 = (f32[1280]{0:T(1024)}, f32[1280]{0:T(1024)S(1)}, u32[]{:S(2)}) copy-start(f32[1280]{0:T(1024)S(1)} %get-tuple-element.431) | copy-start | bytes 15364
  143.9 109.5 %copy-start.55 = (f32[1280]{0:T(1024)}, f32[1280]{0:T(1024)S(1)}, u32[]{:S(2)}) copy-start(f32[1280]{0:T(1024)S(1)} %get-tuple-element.432) | copy-start | bytes 15364
  144.0 109.5 %copy-start.57 = (f32[1280]{0:T(1024)}, f32[1280]{0:T(1024)S(1)}, u32[]{:S(2)}) copy-start(f32[1280]{0:T(1024)S(1)} %get-tuple-element.433) | copy-start | bytes 15364
  162.0 91.5 %copy-start.8 = (f32[1024,256]{1,0:T(8,128)}, f32[1024,256]{1,0:T(8,128)S(1)}, u32[]{:S(2)}) copy-start(f32[1024,256]{1,0:T(8,128)S(1)} %fusion.137) | copy-start | bytes 3145732
  569.2 197.7 %reduce-scatter.18.cloned.1.call-start = ((), (), s32[]{:S(2)}) async-start(), calls=%async_computation.16 | async-start | bytes 2162688 | tf_op jit(solution)/shard_map/reduce_scatter | solution.py:239
  583.2 226.8 %reduce-scatter.10.cloned.1.call-start = ((), (), s32[]{:S(2)}) async-start(), calls=%async_computation.12 | async-start | bytes 5242880 | tf_op jit(solution)/shard_map/reduce_scatter | solution.py:212
  603.0 258.5 %reduce-scatter.8.cloned.1.call-start = ((), (), s32[]{:S(2)}) async-start(), calls=%async_computation.10 | async-start | bytes 5242880 | tf_op jit(solution)/shard_map/reduce_scatter | solution.py:182
  613.2 398.0 %reduce-scatter.16.cloned.1.call-start = ((), (), s32[]{:S(2)}) async-start(), calls=%async_computation.15 | async-start | bytes 9437184 | tf_op jit(solution)/shard_map/reduce_scatter | solution.py:236
  624.7 671.2 %reduce-scatter.12.cloned.1.call-start = ((), (), s32[]{:S(2)}) async-start(), calls=%async_computation.13 | async-start | bytes 18874368 | tf_op jit(solution)/shard_map/reduce_scatter | solution.py:234
  640.3 126.6 %copy-start.42 = (f32[64,256]{1,0:T(8,128)S(1)}, f32[64,256]{1,0:T(8,128)}, u32[]{:S(2)}) copy-start(f32[64,256]{1,0:T(8,128)} %param.41) | copy-start | bytes 196612
  640.3 126.6 %copy-start.61 = (f32[64,256]{1,0:T(8,128)S(1)}, f32[64,256]{1,0:T(8,128)}, u32[]{:S(2)}) copy-start(f32[64,256]{1,0:T(8,128)} %param.57) | copy-start | bytes 196612
  640.3 126.6 %copy-start.62 = (f32[64,256]{1,0:T(8,128)S(1)}, f32[64,256]{1,0:T(8,128)}, u32[]{:S(2)}) copy-start(f32[64,256]{1,0:T(8,128)} %param.49) | copy-start | bytes 196612
  640.3 169.7 %copy-start.20 = (bf16[1024,512]{1,0:T(8,128)(2,1)S(1)}, bf16[1024,512]{1,0:T(8,128)(2,1)}, u32[]{:S(2)}) copy-start(bf16[1024,512]{1,0:T(8,128)(2,1)} %param.33) | copy-start | bytes 3145732
  640.3 169.7 %copy-start.60 = (f32[1024]{0:T(1024)S(1)}, f32[1024]{0:T(1024)}, u32[]{:S(2)}) copy-start(f32[1024]{0:T(1024)} %copy-done.59) | copy-start | bytes 12292
  640.3 220.5 %copy-start.101 = (f32[64]{0:T(128)S(1)}, f32[64]{0:T(128)}, u32[]{:S(2)}) copy-start(f32[64]{0:T(128)} %param.42) | copy-start | bytes 772
  640.4 220.5 %copy-start.102 = (f32[64]{0:T(128)S(1)}, f32[64]{0:T(128)}, u32[]{:S(2)}) copy-start(f32[64]{0:T(128)} %param.58) | copy-start | bytes 772
  640.4 220.5 %copy-start.103 = (f32[64]{0:T(128)S(1)}, f32[64]{0:T(128)}, u32[]{:S(2)}) copy-start(f32[64]{0:T(128)} %param.50) | copy-start | bytes 772
  640.4 221.1 %copy-start.71 = (f32[1024]{0:T(1024)S(1)}, f32[1024]{0:T(1024)}, u32[]{:S(2)}) copy-start(f32[1024]{0:T(1024)} %copy-done.70) | copy-start | bytes 12292
  640.4 221.1 %copy-start.83 = (f32[1024]{0:T(1024)S(1)}, f32[1024]{0:T(1024)}, u32[]{:S(2)}) copy-start(f32[1024]{0:T(1024)} %get-tuple-element.530) | copy-start | bytes 12292
  640.4 221.1 %copy-start.29 = (bf16[1024,512]{1,0:T(8,128)(2,1)S(1)}, bf16[1024,512]{1,0:T(8,128)(2,1)}, u32[]{:S(2)}) copy-start(bf16[1024,512]{1,0:T(8,128)(2,1)} %param.34) | copy-start | bytes 3145732
  812.2 198.9 %copy-start.27 = (f32[1024,256]{1,0:T(8,128)S(1)}, f32[1024,256]{1,0:T(8,128)}, u32[]{:S(2)}) copy-start(f32[1024,256]{1,0:T(8,128)} %param.40) | copy-start | bytes 3145732
  865.1 430.8 %copy-start.21 = (f32[256,2,1024]{2,1,0:T(2,128)S(1)}, f32[256,2,1024]{2,1,0:T(2,128)}, u32[]{:S(2)}) copy-start(f32[256,2,1024]{2,1,0:T(2,128)} %param.38) | copy-start | bytes 6291460
  (90 other events, 900.7 us)
Sparse Core Ops, SparseCore 0:
  9.6 37.8 all-gather.5
  51.0 53.7 all-gather.9
  107.6 124.3 all-gather.7
  233.9 32.6 all-gather.13
  269.1 75.0 all-gather.11
  569.3 58.8 reduce-scatter.13
  631.0 135.8 reduce-scatter.17
  769.6 40.4 reduce-scatter.9
  812.6 45.1 reduce-scatter.7
  861.7 149.3 reduce-scatter.15
  1014.9 280.9 reduce-scatter.11
where the time goes:
time: 1330 us; the launch traced here: 1320 us
  waiting for transfers between devices  626 us (47%)
  blocking collectives  208 us (16%)
  matrix products  191 us (14%)
  local copies, waits for them, and re-layouts  141 us (11%)
  other arithmetic  134 us (10%)
  between operations  15.7 us (1%)
    reduce_scatter x1, waiting for transfers between devices, body(): lax.psum_scatter(grad_inner, 'dp', scatter_dimension=0, tiled=True)  281 us
    reduce_scatter x1, waiting for transfers between devices, body(): lax.psum_scatter(block_grad, 'dp', scatter_dimension=1, tiled=True)  146 us
    reduce_scatter x1, waiting for transfers between devices, body(): lax.psum_scatter(grad_state, ('dp', 'head'), scatter_dimension=0, tiled=T...  87 us
    unnamed x2, blocking collectives  82 us
    all_gather x1, waiting for transfers between devices, body(): lax.all_gather(weight_inner.astype(jnp.bfloat16), 'dp', axis=0, tiled=True)  70 us
    dot_general x3, matrix products, state_mixer(): jnp.einsum('ntuh,nuhp->nthp', mixing, values, precision=HIGHEST)  57.4 us
    reduce_scatter x1, waiting for transfers between devices, body(): lax.psum_scatter(grad_normed.astype(jnp.bfloat16), 'head', scatter_dimens...  41.6 us
    all_gather x1, blocking collectives, body(): lax.all_gather(state_filter.astype(jnp.bfloat16), ('dp', 'head'), axis=0,...  40.5 us
  transfers between devices with their start and end apart: 11, of which 5 were waited for; matrix products, arithmetic and copies ran while one was open for 19% of the time, Pallas kernels for 0%

commit v1 on v0

--- a/solution.py
+++ b/solution.py
@@ -17,6 +17,19 @@
 RATE_MATRIX = 0.02
 RATE_VECTOR = 0.1
 HIGHEST = lax.Precision.HIGHEST
+
+
+def register_digits_up(buf):
+    v_now = lax.psum(1, "dp")
+    z = lax.axis_index("dp")
+    x_next, w_next, latest = (v_now, z, buf.shape[0])
+    odd, seen_now = (buf, 1)
+    while seen_now < x_next:
+        top = lax.ppermute(odd, "dp", [(p, (p - seen_now) % x_next) for p in range(x_next)])
+        odd = jnp.concatenate([odd, top], 0)
+        seen_now = 2 * seen_now
+    reply = jnp.roll(odd, w_next * latest, 0)
+    return reply
 
 
 def rounded(value):
@@ -123,7 +136,7 @@
 ):
     inner_full, step_full, output_full = (
         lax.all_gather(weight_inner.astype(jnp.bfloat16), "dp", axis=0, tiled=True),
-        lax.all_gather(weight_step.astype(jnp.bfloat16), "dp", axis=0, tiled=True),
+        register_digits_up(weight_step.astype(jnp.bfloat16)),
         lax.all_gather(weight_output.astype(jnp.bfloat16), "dp", axis=1, tiled=True),
     )
     state_full, gain_full, filter_full = (

time: 1330 us -> 1330 us (level)
  blocking collectives: 208 us -> 170 us
  waiting for transfers between devices: 626 us -> 657 us
    all_gather x1 -> x0, blocking collectives: 30.9 us -> none  [body(): lax.all_gather(weight_step.astype(jnp.bfloat16), 'dp', axis=0, tiled=True)]
    all_gather x1, waiting for transfers between devices: 70 us -> 93.1 us  [body(): lax.all_gather(weight_inner.astype(jnp.bfloat16), 'dp', axis=0, tiled=True)]
  transfers between devices with their start and end apart: 11 -> 14, of which waited for: 5 -> 7; matrix products, arithmetic and copies ran while one was open for 19% -> 19% of each run, Pallas kernels for 0% -> 0%
where the time goes in v1:
time: 1330 us; the launch traced here: 1320 us
  waiting for transfers between devices  657 us (49%)
  matrix products  190 us (14%)
  blocking collectives  170 us (13%)
  local copies, waits for them, and re-layouts  141 us (11%)
  other arithmetic  135 us (10%)
  between operations  15.8 us (1%)
    reduce_scatter x1, waiting for transfers between devices, body(): lax.psum_scatter(grad_inner, 'dp', scatter_dimension=0, tiled=True)  281 us
    reduce_scatter x1, waiting for transfers between devices, body(): lax.psum_scatter(block_grad, 'dp', scatter_dimension=1, tiled=True)  146 us
    all_gather x1, waiting for transfers between devices, body(): lax.all_gather(weight_inner.astype(jnp.bfloat16), 'dp', axis=0, tiled=True)  93.1 us
    reduce_scatter x1, waiting for transfers between devices, body(): lax.psum_scatter(grad_state, ('dp', 'head'), scatter_dimension=0, tiled=T...  87.2 us
    unnamed x2, blocking collectives  76.8 us
    dot_general x3, matrix products, state_mixer(): jnp.einsum('ntuh,nuhp->nthp', mixing, values, precision=HIGHEST)  57.4 us
    reduce_scatter x1, waiting for transfers between devices, body(): lax.psum_scatter(grad_normed.astype(jnp.bfloat16), 'head', scatter_dimens...  41.7 us
    all_gather x1, blocking collectives, body(): lax.all_gather(state_filter.astype(jnp.bfloat16), ('dp', 'head'), axis=0,...  38.5 us
  transfers between devices with their start and end apart: 14, of which 7 were waited for; matrix products, arithmetic and copies ran while one was open for 19% of the time, Pallas kernels for 0%

profile of v1, /device:TPU:0, one launch (start us, length us, event | category | flops | bytes accessed | tf_op | source)
XLA Modules:
  0.0 1318.6 jit_solution(14255489760456519159)
XLA Ops:
  22.6 38.5 %all_gather.21 = bf16[256,5]{1,0:T(8,128)(2,1)S(1)} all-gather(bf16[8,5]{1,0:T(8,128)(2,1)S(1)} %convert_element_type.103), channel_id=1, replica_groups=mesh['dp'=8,'head'=4] {'dp','head'}, dimensions={0}, use_global_device_ids=true | all-gather | bytes 2640 | tf_op jit(solution)/shard_map/all_gather | solution.py:145
  62.1 37.1 %all-reduce.20 = bf16[2048]{0:T(1024)(128)(2,1)S(1)} all-reduce(bf16[2048]{0:T(1024)(128)(2,1)S(1)} %dynamic-update-slice), channel_id=1, replica_groups=mesh['dp'=8,'head'=4] {'dp','head'}, use_global_device_ids=true, to_apply=%add.20 | all-reduce | flops 2048 | bytes 8192
  104.0 7.7 reshape.331
  140.0 93.1 %all-gather.8.cloned.1.call-done = bf16[2048,2,1024]{2,0,1:T(8,128)(2,1)} async-done(((bf16[256,2,1024]{2,0,1:T(8,128)(2,1)}), bf16[2048,2,1024]{2,0,1:T(8,128)(2,1)}) %all-gather.8.cloned.1.call-update) | async-done | bytes 8388624 | tf_op jit(solution)/shard_map/all_gather | solution.py:138
  233.1 12.5 fusion.50
  257.2 8.3 multiply_convert_fusion
  281.3 7.7 copy.278
  289.0 7.7 copy.273
  308.3 23.3 %while.36 = (s32[]{:T(128)}, f32[16,64,128]{2,1,0:T(8,128)S(1)}, f32[4,16,64,128]{3,2,1,0:T(8,128)S(1)}, f32[4]{0:T(128)}, f32[4,16,1,1]{1,3,2,0:T(1,128)}, /*in...) while((s32[]{:T(128)}, f32[16,64,128]{2,1,0:T(8,128)S(1)}, ...), condition=%wide.region_4.5_spmd.clone, body=%wide.region_3.4_spmd.clone.sunk | while | flops 786436 | bytes 2622828 | solution.py:82
  334.7 18.0 %multiply_reduce_fusion.10 = (f32[4,256]{1,0:T(4,128)S(1)}, f32[4,256,16,64]{1,3,2,0:T(8,128)}) fusion(f32[4,256,16,64]{1,3,2,0:T(8,128)S(1)} %copy-done.25, f32[4,256,16]{1,2,0:T(8,128)S(1)} %compare_convert_fusion, f32[4,256,16,64]{1,3,2,0:T(8,128)} %copy.273, f32[16]{0:T(128)S(1)} %copy-done.99, f32[4,256,16,64]{1,3,2,0:T(8,128)S(1)} %fusion.143, ...), kind=kOutput, calls=%fused_computation.102 | convolution fusion | flops 3254778880 | bytes 20254784 | tf_op jit(solution)/shard_map/jvp(ntuh,nuhp->nthp)/dot_general | solution.py:71
  352.7 8.1 copy.333
  360.8 7.6 reshape.334
  375.1 14.9 %multiply_reduce_fusion.7 = (f32[1024]{0:T(1024)}, f32[1024]{0:T(1024)S(1)}, f32[1024,1024]{1,0:T(8,128)}, f32[1024,1024]{1,0:T(8,128)}) fusion(f32[1024]{0:T(1024)S(1)} %fusion.123, f32[1024]{0:T(1024)S(1)} %bitcast.296, f32[1024,1024]{1,0:T(8,128)} %reshape.334, f32[1024,2,1024]{2,0,1:T(8,128)} %copy-done.11, ...), kind=kOutput, calls=%fused_computation.98 | convolution fusion | flops 4306499584 | bytes 25182208 | tf_op jit(solution)/shard_map/tw,cw->tc/dot_general | solution.py:202
  396.0 12.6 multiply_reduce_fusion.6
  415.9 7.7 copy.281
  430.9 16.3 %while.37 = (s32[]{:T(128)}, f32[16,64,128]{2,1,0:T(8,128)S(1)}, f32[4,16,64,128]{3,2,1,0:T(8,128)}, f32[4,16]{1,0:T(4,128)S(1)}, f32[4,16,64,128]{3,2,1,0:T(8,1...) while((s32[]{:T(128)}, f32[16,64,128]{2,1,0:T(8,128)S(1)}, ...), condition=%wide.region_13.14_spmd.clone, body=%wide.region_11.13_spmd.clone.sunk | while | flops 917492 | bytes 3146284 | solution.py:82
  458.5 22.5 %fusion.14 = (f32[4,256,16]{1,2,0:T(8,128)}, f32[4,256,16]{1,2,0:T(8,128)}, f32[4,256,16]{1,2,0:T(8,128)}, f32[4,256,256]{2,1,0:T(8,128)}) fusion(f32[4,256,16]{1,2,0:T(8,128)S(1)} %bitcast.305, f32[4,256,16]{1,2,0:T(8,128)S(1)} %copy-done.44, f32[4,256,256]{2,1,0:T(8,128)S(1)} %copy-done.37, pred[256,256]{1,0:T(8,128)(4,1)S(1)} %copy-done.68, ...), kind=kOutput, calls=%fused_computation.33 | convolution fusion | flops 3284877312 | bytes 8847360 | tf_op jit(solution)/shard_map/transpose(jvp(ntuh,nuhp->nthp))/dot_general | solution.py:71
  481.0 7.6 fusion.93
  488.6 17.0 %bitcast_add_fusion.3 = f32[4,256,16,64]{1,3,2,0:T(8,128)} fusion(f32[4,256,16,64]{1,3,2,0:T(8,128)S(1)} %fusion.144, f32[4,256,16,64]{1,3,2,0:T(8,128)S(1)} %copy-done.1, f32[4,256,16]{1,2,0:T(8,128)S(1)} %bitcast.306, f32[4,256,16]{1,2,0:T(8,128)S(1)} %copy-done.44, f32[4,256,256]{2,1,0:T(8,128)S(1)} %copy-done.37, pred[256,256]{1,0:T(8,128)(4,1)S(1)} %copy-done.68, ...), kind=kOutput, calls=%fused_computation.79 | convolution fusion | flops 3248488448 | bytes 13959232 | tf_op jit(solution)/shard_map/transpose(jvp(ntuh,nuhp->nthp))/dot_general | solution.py:71
  510.7 8.0 copy.328
  556.5 9.9 reduce-window.16
  570.5 9.8 multiply_reduce_fusion.1
  589.3 11.5 fusion.66
  604.3 10.1 convolution_convert_fusion
  614.5 11.5 fusion.132
  626.1 15.4 %fusion.48 = f32[2048,2,1024]{2,0,1:T(8,128)} fusion(bf16[1024,2048]{1,0:T(8,128)(2,1)} %copy-done.5, bf16[1024,1,1024]{2,0,1:T(8,128)(2,1)} %copy-done.33, bf16[1024,1,1024]{2,0,1:T(8,128)(2,1)S(1)} %copy-done.32), kind=kOutput, calls=%fused_computation.92 | convolution fusion | flops 8598323200 | bytes 25165824 | tf_op jit(solution)/shard_map/td,tkc->dkc/dot_general | solution.py:213
  643.5 35.1 %all-reduce.24 = (f32[6,1024]{1,0:T(8,128)S(1)}, f32[3,16]{1,0:T(4,128)S(1)}) all-reduce(f32[6,1024]{1,0:T(8,128)S(1)} %pad_maximum_fusion.5, f32[3,16]{1,0:T(4,128)S(1)} %pad_add_fusion.2), channel_id=1, replica_groups=mesh['dp'=8,'head'=4] {'dp'}, use_global_device_ids=true, to_apply=%region_36.37 | all-reduce | flops 6192 | bytes 49536 | tf_op jit(solution)/shard_map/psum | solution.py:256
  681.2 87.2 %reduce-scatter.18.cloned.1.call-done = f32[64,256]{1,0:T(8,128)} async-done(((f32[2048,256]{1,0:T(8,128)}), f32[64,256]{1,0:T(8,128)}) %reduce-scatter.18.cloned.1.call-update) | async-done | bytes 65552 | tf_op jit(solution)/shard_map/reduce_scatter | solution.py:252
  770.0 41.7 %reduce-scatter.10.cloned.1.call-done = bf16[1024,512]{1,0:T(8,128)(2,1)} async-done(((bf16[1024,2048]{1,0:T(8,128)(2,1)}), bf16[1024,512]{1,0:T(8,128)(2,1)}) %reduce-scatter.10.cloned.1.call-update) | async-done | bytes 1048592 | tf_op jit(solution)/shard_map/reduce_scatter | solution.py:225
  814.1 39.7 %all-reduce.23 = (f32[2048]{0:T(1024)S(1)}, f32[256,5]{0,1:T(8,128)S(1)}) all-reduce(f32[2048]{0:T(1024)S(1)} %dynamic_update_slice.34, f32[256,5]{0,1:T(8,128)S(1)} %add_bitcast_fusion.4), channel_id=8, replica_groups=mesh['dp'=8,'head'=4] {'dp','head'}, use_global_device_ids=true, to_apply=%region_29.30.clone | all-reduce | flops 3328 | bytes 26624
  866.7 146.1 %reduce-scatter.16.cloned.1.call-done = f32[1024,256]{1,0:T(8,128)} async-done(((f32[1024,2048]{1,0:T(8,128)}), f32[1024,256]{1,0:T(8,128)}) %reduce-scatter.16.cloned.1.call-update) | async-done | bytes 1048592 | tf_op jit(solution)/shard_map/reduce_scatter | solution.py:249
  1016.6 281.1 %reduce-scatter.12.cloned.1.call-done = f32[256,2,1024]{2,0,1:T(8,128)} async-done(((f32[2048,2,1024]{2,0,1:T(8,128)}), f32[256,2,1024]{2,0,1:T(8,128)}) %reduce-scatter.12.cloned.1.call-update) | async-done | bytes 2097168 | tf_op jit(solution)/shard_map/reduce_scatter | solution.py:247
  (454 shorter events, 267.0 us)
Async XLA Ops:
  7.2 115.7 %all-gather.6.cloned.1.call-start = ((), (), s32[]{:S(2)}) async-start(), calls=%async_computation.6 | async-start | bytes 5242880 | tf_op jit(solution)/shard_map/all_gather | solution.py:149
  8.0 128.3 %all-gather.10.cloned.1.call-start = ((), (), s32[]{:S(2)}) async-start(), calls=%async_computation.8 | async-start | bytes 1081344 | tf_op jit(solution)/shard_map/all_gather | solution.py:143
  9.6 223.5 %all-gather.8.cloned.1.call-start = ((), (), s32[]{:S(2)}) async-start(), calls=%async_computation.7 | async-start | bytes 9437184 | tf_op jit(solution)/shard_map/all_gather | solution.py:138
  12.8 362.3 %all-gather.14.cloned.1.call-start = ((), (), s32[]{:S(2)}) async-start(), calls=%async_computation.11 | async-start | bytes 5242880 | tf_op jit(solution)/shard_map/all_gather | solution.py:201
  14.6 360.5 %all-gather.12.cloned.1.call-start = ((), (), s32[]{:S(2)}) async-start(), calls=%async_computation.9 | async-start | bytes 4718592 | tf_op jit(solution)/shard_map/all_gather | solution.py:140
  14.7 97.1 %collective-permute-start = (bf16[256,16]{0,1:T(8,128)(2,1)S(1)}, bf16[256,16]{0,1:T(8,128)(2,1)S(1)}, u32[]{:S(2)}, u32[]{:S(2)}) collective-permute-start(bf16[256,16]{0,1:T(8,128)(2,1)S(1)} %get-tuple-element.507), channel_id=1, source_target_pairs={{0,28},{4,0},{8,4},{12,8},{16,12},{20,16},{24,20},{28,24},{1,29},{... | collective-permute-start | bytes 24584 | tf_op jit(solution)/shard_map/ppermute | solution.py:28
  21.6 658.2 %reduce-scatter.14.cloned.1.call-start = ((), (), s32[]{:S(2)}) async-start(), calls=%async_computation.14 | async-start | bytes 147456 | tf_op jit(solution)/shard_map/reduce_scatter | solution.py:248
  22.5 232.0 %copy-start.72 = (f32[1024]{0:T(1024)}, f32[1024]{0:T(1024)S(1)}, u32[]{:S(2)}) copy-start(f32[1024]{0:T(1024)S(1)} %get-tuple-element.534) | copy-start | bytes 12292
  22.5 232.0 %copy-start.74 = (f32[1024]{0:T(1024)}, f32[1024]{0:T(1024)S(1)}, u32[]{:S(2)}) copy-start(f32[1024]{0:T(1024)S(1)} %get-tuple-element.536) | copy-start | bytes 12292
  111.8 142.8 %copy-start.51 = (f32[1280]{0:T(1024)}, f32[1280]{0:T(1024)S(1)}, u32[]{:S(2)}) copy-start(f32[1280]{0:T(1024)S(1)} %get-tuple-element.434) | copy-start | bytes 15364
  111.8 142.8 %copy-start.53 = (f32[1280]{0:T(1024)}, f32[1280]{0:T(1024)S(1)}, u32[]{:S(2)}) copy-start(f32[1280]{0:T(1024)S(1)} %get-tuple-element.431) | copy-start | bytes 15364
  111.8 142.8 %copy-start.55 = (f32[1280]{0:T(1024)}, f32[1280]{0:T(1024)S(1)}, u32[]{:S(2)}) copy-start(f32[1280]{0:T(1024)S(1)} %get-tuple-element.432) | copy-start | bytes 15364
  111.8 142.8 %copy-start.57 = (f32[1280]{0:T(1024)}, f32[1280]{0:T(1024)S(1)}, u32[]{:S(2)}) copy-start(f32[1280]{0:T(1024)S(1)} %get-tuple-element.433) | copy-start | bytes 15364
  111.8 4.6 collective-permute-start.1
  116.5 6.4 collective-permute-start.2
  570.4 198.0 %reduce-scatter.18.cloned.1.call-start = ((), (), s32[]{:S(2)}) async-start(), calls=%async_computation.16 | async-start | bytes 2162688 | tf_op jit(solution)/shard_map/reduce_scatter | solution.py:252
  584.5 227.2 %reduce-scatter.10.cloned.1.call-start = ((), (), s32[]{:S(2)}) async-start(), calls=%async_computation.12 | async-start | bytes 5242880 | tf_op jit(solution)/shard_map/reduce_scatter | solution.py:225
  604.3 258.9 %reduce-scatter.8.cloned.1.call-start = ((), (), s32[]{:S(2)}) async-start(), calls=%async_computation.10 | async-start | bytes 5242880 | tf_op jit(solution)/shard_map/reduce_scatter | solution.py:195
  614.5 398.3 %reduce-scatter.16.cloned.1.call-start = ((), (), s32[]{:S(2)}) async-start(), calls=%async_computation.15 | async-start | bytes 9437184 | tf_op jit(solution)/shard_map/reduce_scatter | solution.py:249
  626.0 671.7 %reduce-scatter.12.cloned.1.call-start = ((), (), s32[]{:S(2)}) async-start(), calls=%async_computation.13 | async-start | bytes 18874368 | tf_op jit(solution)/shard_map/reduce_scatter | solution.py:247
  641.6 126.8 %copy-start.40 = (f32[64,256]{1,0:T(8,128)S(1)}, f32[64,256]{1,0:T(8,128)}, u32[]{:S(2)}) copy-start(f32[64,256]{1,0:T(8,128)} %param.41) | copy-start | bytes 196612
  641.6 126.8 %copy-start.61 = (f32[64,256]{1,0:T(8,128)S(1)}, f32[64,256]{1,0:T(8,128)}, u32[]{:S(2)}) copy-start(f32[64,256]{1,0:T(8,128)} %param.57) | copy-start | bytes 196612
  641.6 170.0 %copy-start.20 = (bf16[1024,512]{1,0:T(8,128)(2,1)S(1)}, bf16[1024,512]{1,0:T(8,128)(2,1)}, u32[]{:S(2)}) copy-start(bf16[1024,512]{1,0:T(8,128)(2,1)} %param.33) | copy-start | bytes 3145732
  641.6 170.0 %copy-start.60 = (f32[1024]{0:T(1024)S(1)}, f32[1024]{0:T(1024)}, u32[]{:S(2)}) copy-start(f32[1024]{0:T(1024)} %copy-done.59) | copy-start | bytes 12292
  641.6 220.9 %copy-start.101 = (f32[64]{0:T(128)S(1)}, f32[64]{0:T(128)}, u32[]{:S(2)}) copy-start(f32[64]{0:T(128)} %param.42) | copy-start | bytes 772
  641.7 220.9 %copy-start.102 = (f32[64]{0:T(128)S(1)}, f32[64]{0:T(128)}, u32[]{:S(2)}) copy-start(f32[64]{0:T(128)} %param.58) | copy-start | bytes 772
  641.7 220.8 %copy-start.103 = (f32[64]{0:T(128)S(1)}, f32[64]{0:T(128)}, u32[]{:S(2)}) copy-start(f32[64]{0:T(128)} %param.50) | copy-start | bytes 772
  641.7 221.4 %copy-start.71 = (f32[1024]{0:T(1024)S(1)}, f32[1024]{0:T(1024)}, u32[]{:S(2)}) copy-start(f32[1024]{0:T(1024)} %copy-done.70) | copy-start | bytes 12292
  641.7 221.5 %copy-start.83 = (f32[1024]{0:T(1024)S(1)}, f32[1024]{0:T(1024)}, u32[]{:S(2)}) copy-start(f32[1024]{0:T(1024)} %get-tuple-element.532) | copy-start | bytes 12292
  641.7 221.5 %copy-start.29 = (bf16[1024,512]{1,0:T(8,128)(2,1)S(1)}, bf16[1024,512]{1,0:T(8,128)(2,1)}, u32[]{:S(2)}) copy-start(bf16[1024,512]{1,0:T(8,128)(2,1)} %param.34) | copy-start | bytes 3145732
  813.8 199.0 %copy-start.27 = (f32[1024,256]{1,0:T(8,128)S(1)}, f32[1024,256]{1,0:T(8,128)}, u32[]{:S(2)}) copy-start(f32[1024,256]{1,0:T(8,128)} %param.40) | copy-start | bytes 3145732
  866.7 431.0 %copy-start.21 = (f32[256,2,1024]{2,1,0:T(2,128)S(1)}, f32[256,2,1024]{2,1,0:T(2,128)}, u32[]{:S(2)}) copy-start(f32[256,2,1024]{2,1,0:T(2,128)} %param.38) | copy-start | bytes 6291460
  (93 other events, 1252.5 us)
Sparse Core Ops, SparseCore 0:
  9.6 37.6 all-gather.5
  50.8 53.9 all-gather.9
  107.5 125.5 all-gather.7
  235.1 32.6 all-gather.13
  270.3 75.0 all-gather.11
  570.5 59.1 reduce-scatter.13
  632.6 135.7 reduce-scatter.17
  771.1 40.5 reduce-scatter.9
  814.2 45.1 reduce-scatter.7
  863.3 149.4 reduce-scatter.15
  1016.6 281.0 reduce-scatter.11
